TPU v7x, 32 devices: a whole 2x2x4 slice. The times are simulated.
32 devices in a mesh: parts: 2 (over y), row: 4 (over z), col: 4 (over x, core).
Axes of the slice: x: 2, y: 2, z: 4, core: 2. Of those that a mesh axis runs over, the one named last changes fastest.
Arguments:
- amplitudes: bfloat16 [8, 100, 512, 512], P('parts', 'col', 'row'), parts along dimension 0, may hold values from -12 to 12
- integrals: bfloat16 [200, 512, 512], P(('parts', 'col'), 'row'), parts along dimension 0, may hold values from -0.109375 to 0.109375
- occ_irrep: int32 [200], P('parts'), parts along dimension 0, may hold values from 0 to 7, as said below
- vir_irrep: int32 [1024], P('parts'), parts along dimension 0, may hold values from 0 to 7, as said below
- screen: int32 [200, 8], P('parts'), parts along dimension 0, may hold values 0 or 1
- occ_energy: float32 [200], P('parts'), parts along dimension 0, may hold values from -1 to -0.3
- vir_energy: float32 [1024], P('parts'), parts along dimension 0, may hold values from 0.1 to 1
Outputs:
- update: float32 [512, 8, 512], P('row', 'parts', 'col'), parts along dimension 1
There are 2 independent parts, one for each index of `parts`. A program takes and returns all parts, laid end to end along the dimension named above; each array names one. Nothing has to cross between parts.
Inputs may be any that keep to these rules, and one draw needn't show every extreme that they name: `occ_irrep`: the labels never fall from one orbital to the next; the first is 0 and the last is 7. `vir_irrep`: the labels never fall from one orbital to the next and every label from 0 to 7 occurs; exactly one label covers 256 virtual orbitals, every other label fewer.
All inputs are finite; a program needn't handle non-finite values.
Results may differ from a plain program's by a relative error of at most 0.0003.
Values may be sent and summed in bfloat16 or wider, within the bound.
A program may use at most 128 MiB of HBM per device.

v0:
```python
import jax
import jax.numpy as jnp
from jax import lax
from jax.sharding import PartitionSpec as P


def folded_integrals(integrals, occ_local, vir_local, vir_irrep, screen_rows, pair_label):
    half = vir_irrep.shape[0] // 2
    irrep_codes = jnp.arange(8, dtype=jnp.int32)
    screen_local = jnp.sum(
        screen_rows[:, None, :] * (vir_local[None, :, None] == irrep_codes).astype(jnp.int32),
        axis=2,
    )
    wanted = jnp.bitwise_xor(jnp.bitwise_xor(occ_local[:, None], vir_local[None, :]), pair_label)
    wanted = jnp.where(screen_local == 1, wanted, -1)[:, :, None]
    zeros = jnp.zeros((), integrals.dtype)
    low = jnp.where(wanted == vir_irrep[None, None, :half], integrals[:, :, :half], zeros)
    return jnp.where(wanted == vir_irrep[None, None, half:], integrals[:, :, half:], low)


def on_device(amplitudes, integrals, occ_irrep, vir_irrep, screen, occ_energy, vir_energy):
    row_count = lax.axis_size("row")
    column_count = lax.axis_size("col")
    row, col = (lax.axis_index("row"), lax.axis_index("col"))
    batch_size, occ_share, vir_share, vir_total = amplitudes.shape
    half = vir_total // 2
    vir_columns = vir_total // column_count
    occ_offset = col * occ_share
    occ_local = lax.dynamic_slice_in_dim(occ_irrep, occ_offset, occ_share)
    vir_local = lax.dynamic_slice_in_dim(vir_irrep, row * vir_share, vir_share)
    screen_rows = lax.dynamic_slice_in_dim(screen, occ_offset, occ_share, 0)
    pair_label = occ_irrep[batch_size]
    folded = folded_integrals(integrals, occ_local, vir_local, vir_irrep, screen_rows, pair_label)
    gathered = lax.all_gather(folded, "row", axis=1, tiled=True)
    shift = jnp.bitwise_xor(occ_irrep[:batch_size, None], occ_local[None, :])
    keep_amp = (
        jnp.bitwise_xor(shift[:, :, None], vir_local[None, None, :])[:, :, :, None]
        == vir_irrep[None, None, None, :]
    )
    amp_kept = jnp.where(keep_amp, amplitudes, jnp.zeros_like(amplitudes))
    partial = lax.dot_general(
        amp_kept, gathered, (((1, 3), (0, 1)), ((), ())), preferred_element_type=jnp.float32
    )
    if row_count == column_count and column_count == 4:
        piece = lax.psum_scatter(partial, "col", scatter_dimension=2, tiled=True)
        routes = []
        for flip in (0, 1):
            pairs = []
            for r in range(row_count):
                for q in range(column_count):
                    target = q // 2 + 2 * ((q + flip) % 2)
                    pairs.append((r * column_count + q, target * column_count + r))
            routes.append(lax.ppermute(piece, ("row", "col"), pairs))
        swap = row // 2 == 1
        first = jnp.where(swap, routes[1], routes[0])
        second = jnp.where(swap, routes[0], routes[1])
        cycle = jnp.concatenate([first, second], axis=2)
    else:
        whole = lax.all_gather(lax.psum(partial, "col"), "row", axis=1, tiled=True)
        cycle = lax.dynamic_slice_in_dim(whole, col * vir_columns, vir_columns, 1)
        cycle = lax.dynamic_slice_in_dim(cycle, row * vir_share % half, vir_share, 2)
    cycle = jnp.transpose(cycle, (2, 0, 1))
    col_irrep = lax.dynamic_slice_in_dim(vir_irrep, col * vir_columns, vir_columns)
    kept = (
        jnp.bitwise_xor(occ_irrep[:batch_size, None], pair_label ^ col_irrep[None, :])[None]
        == vir_local[:, None, None]
    )
    cycle = jnp.where(kept, cycle, 0.0)
    energy_cols = lax.dynamic_slice_in_dim(vir_energy, col * vir_columns, vir_columns)
    energy_rows = lax.dynamic_slice_in_dim(vir_energy, row * vir_share, vir_share)
    denominator = (
        occ_energy[:batch_size][None, :, None]
        + occ_energy[batch_size]
        - energy_cols[None, None, :]
        - energy_rows[:, None, None]
    )
    return cycle / denominator


def solution(mesh):
    in_specs = (
        P("parts", "col", "row", None),
        P(("parts", "col"), "row", None),
        P("parts"),
        P("parts"),
        P("parts", None),
        P("parts"),
        P("parts"),
    )
    out_specs = P("row", "parts", "col")
    return jax.shard_map(
        on_device, mesh=mesh, in_specs=in_specs, out_specs=out_specs, check_vma=False
    )
```

profile of v0, /device:TPU:2, one launch (start us, length us, event | category | flops | bytes accessed | tf_op | source)
XLA Modules:
  0.0 192.5 jit_solution(17666716235107848208)
XLA Ops:
  6.5 0.0 copy-start
  6.5 0.0 all-gather.2.cloned.1.call-start
  6.5 1.2 slice.26
  7.8 0.8 fusion.14
  8.5 1.5 dynamic-slice_xor_fusion
  10.0 0.7 dynamic_slice.20
  10.8 0.0 copy-done
  10.8 0.1 constant_dynamic-slice_fusion
  10.8 0.1 copy.12
  10.9 3.4 %fusion.12 = (bf16[25,128,256]{2,1,0:T(8,128)(2,1)}, bf16[25,128,256]{2,1,0:T(8,128)(2,1)S(1)}) fusion(bf16[25,128,512]{2,1,0:T(8,128)(2,1)} %param.8), kind=kLoop, calls=%fused_computation.26 | loop fusion | bytes 6553600 | tf_op jit(solution)/shard_map/slice | solution.py:17
  14.4 2.1 %copy.17 = bf16[25,128,256]{1,2,0:T(8,128)(2,1)S(1)} copy(bf16[25,128,256]{2,1,0:T(8,128)(2,1)S(1)} %get-tuple-element.6) | data formatting | bytes 3276800
  16.5 3.1 %copy.18 = bf16[25,128,256]{1,2,0:T(8,128)(2,1)S(1)} copy(bf16[25,128,256]{2,1,0:T(8,128)(2,1)} %get-tuple-element.5) | data formatting | bytes 3276800
  19.6 0.1 multiply_reduce_fusion
  19.7 0.7 xor_select_fusion
  20.4 0.0 copy-start.2
  20.4 0.0 copy-start.1
  20.4 2.1 %compare_select_fusion.3 = bf16[25,128,256]{1,2,0:T(8,128)(2,1)} fusion(bf16[25,128,256]{1,2,0:T(8,128)(2,1)S(1)} %copy.17, bf16[25,128,256]{1,2,0:T(8,128)(2,1)S(1)} %copy.18, s32[25,128]{1,0:T(8,128)S(1)} %xor_select_fusion, s32[256]{0:T(256)S(1)} %get-tuple-element.14, s32[256]{0:T(256)S(1)} %get-tuple-element.13), kind=kLoop, calls=%fused_computation.7 | loop fusion | flops 3276800 | bytes 4930048 | tf_op jit(solution)/shard_map/jit(_where)/select_n | solution.py:18
  22.5 0.0 all-gather.2.cloned.1.call-update
  22.5 0.0 reduce-scatter.2.cloned.1.call-start
  22.6 0.0 copy-done.2
  22.6 0.1 broadcast_xor_fusion.1
  22.6 0.1 broadcast_xor_fusion
  22.7 0.0 copy-done.1
  22.7 10.7 %compare_select_fusion.8 = bf16[4,25,128,512]{3,2,1,0:T(8,128)(2,1)} fusion(bf16[4,25,128,512]{3,2,1,0:T(8,128)(2,1)} %param.7, s32[512]{0:T(512)S(1)} %copy-done.1, s32[4,25,128]{2,1,0:T(8,128)S(1)} %broadcast_xor_fusion), kind=kLoop, calls=%fused_computation.clone.clone.clone.clone.1 | loop fusion | flops 13107200 | bytes 26267648 | tf_op jit(solution)/shard_map/dot_general | solution.py:41
  33.4 0.0 copy-start.4
  33.4 0.0 copy-start.3
  33.4 109.6 %all-gather.2.cloned.1.call-done = bf16[25,512,256]{1,2,0:T(8,128)(2,1)} async-done(((bf16[25,128,256]{1,2,0:T(8,128)(2,1)}), bf16[25,512,256]{1,2,0:T(8,128)(2,1)}) %all-gather.2.cloned.1.call-update) | async-done | bytes 6553616 | tf_op jit(solution)/shard_map/all_gather | solution.py:34
  143.0 9.2 %fusion.5 = f32[4,128,256]{1,2,0:T(8,128)} fusion(bf16[25,512,256]{1,2,0:T(8,128)(2,1)} %all-gather.2.cloned.1.call-done, bf16[4,25,128,512]{3,2,1,0:T(8,128)(2,1)} %compare_select_fusion.8), kind=kOutput, calls=%fused_computation.8 | convolution fusion | flops 3355443200 | bytes 20185088 | tf_op jit(solution)/shard_map/dot_general | solution.py:41
  152.2 0.0 reduce-scatter.2.cloned.1.call-update
  152.3 0.0 copy-done.4
  152.3 0.6 slice.32
  152.9 0.0 copy-done.3
  152.9 0.1 fusion.13
  153.0 0.6 slice_add_fusion
  153.6 0.1 broadcast_xor_fusion.2
  153.7 17.4 %reduce-scatter.2.cloned.1.call-done = f32[4,128,64]{1,2,0:T(8,128)} async-done(((f32[4,128,256]{1,2,0:T(8,128)}), f32[4,128,64]{1,2,0:T(8,128)}) %reduce-scatter.2.cloned.1.call-update) | async-done | bytes 131088 | tf_op jit(solution)/shard_map/reduce_scatter | solution.py:45
  171.1 4.5 %collective-permute-start = (f32[4,128,64]{1,2,0:T(8,128)}, f32[4,128,64]{1,2,0:T(8,128)S(1)}, u32[]{:S(2)}, u32[]{:S(2)}) collective-permute-start(f32[4,128,64]{1,2,0:T(8,128)} %reduce-scatter.2.cloned.1.call-done), channel_id=1, source_target_pairs={{0,8},{1,0},{2,12},{3,4},{4,9},{5,1},{6,13},{7,5},{8,10},{9,2},{10... | collective-permute-start | bytes 393224 | tf_op jit(solution)/shard_map/ppermute | solution.py:53
  175.6 1.9 collective-permute-start.1
  177.5 0.1 broadcast_subtract_fusion
  177.6 1.5 collective-permute-done
  179.0 5.6 %collective-permute-done.1 = f32[4,128,64]{1,2,0:T(8,128)S(1)} collective-permute-done((f32[4,128,64]{1,2,0:T(8,128)}, f32[4,128,64]{1,2,0:T(8,128)S(1)}, u32[]{:S(2)}, u32[]{:S(2)}) %collective-permute-start.1) | collective-permute-done | bytes 131104 | tf_op jit(solution)/shard_map/ppermute | solution.py:53
  184.7 0.1 fusion.9
  184.8 0.9 copy.15
  (2 shorter events, 0.0 us)
Async XLA Ops:
  6.5 4.2 %copy-start = (s32[100,8]{0,1:T(8,128)S(1)}, s32[100,8]{0,1:T(8,128)}, u32[]{:S(2)}) copy-start(s32[100,8]{0,1:T(8,128)} %param.11) | copy-start | bytes 9604
  6.5 136.5 %all-gather.2.cloned.1.call-start = ((), (), s32[]{:S(2)}) async-start(), calls=%async_computation.1 | async-start | bytes 8192000 | tf_op jit(solution)/shard_map/all_gather | solution.py:34
  20.4 2.1 %copy-start.2 = (s32[100]{0:T(128)S(1)}, s32[100]{0:T(128)}, u32[]{:S(2)}) copy-start(s32[100]{0:T(128)} %param.9) | copy-start | bytes 1204
  20.4 2.3 %copy-start.1 = (s32[512]{0:T(512)S(1)}, s32[512]{0:T(512)}, u32[]{:S(2)}) copy-start(s32[512]{0:T(512)} %param.10) | copy-start | bytes 6148
  22.5 148.6 %reduce-scatter.2.cloned.1.call-start = ((), (), s32[]{:S(2)}) async-start(), calls=%async_computation.2 | async-start | bytes 655360 | tf_op jit(solution)/shard_map/reduce_scatter | solution.py:45
  33.4 118.8 %copy-start.4 = (f32[100]{0:T(128)S(1)}, f32[100]{0:T(128)}, u32[]{:S(2)}) copy-start(f32[100]{0:T(128)} %param.12) | copy-start | bytes 1204
  33.4 119.4 %copy-start.3 = (f32[512]{0:T(512)S(1)}, f32[512]{0:T(512)}, u32[]{:S(2)}) copy-start(f32[512]{0:T(512)} %param.13) | copy-start | bytes 6148
  171.1 7.9 %collective-permute-start = (f32[4,128,64]{1,2,0:T(8,128)}, f32[4,128,64]{1,2,0:T(8,128)S(1)}, u32[]{:S(2)}, u32[]{:S(2)}) collective-permute-start(f32[4,128,64]{1,2,0:T(8,128)} %reduce-scatter.2.cloned.1.call-done), channel_id=1, source_target_pairs={{0,8},{1,0},{2,12},{3,4},{4,9},{5,1},{6,13},{7,5},{8,10},{9,2},{10... | collective-permute-start | bytes 393224 | tf_op jit(solution)/shard_map/ppermute | solution.py:53
  175.6 9.0 %collective-permute-start.1 = (f32[4,128,64]{1,2,0:T(8,128)}, f32[4,128,64]{1,2,0:T(8,128)S(1)}, u32[]{:S(2)}, u32[]{:S(2)}) collective-permute-start(f32[4,128,64]{1,2,0:T(8,128)} %reduce-scatter.2.cloned.1.call-done), channel_id=1, source_target_pairs={{0,0},{1,8},{2,4},{3,12},{4,1},{5,9},{6,5},{7,13},{8,2},{9,10},{10... | collective-permute-start | bytes 393224 | tf_op jit(solution)/shard_map/ppermute | solution.py:53
Sparse Core Ops, SparseCore 0:
  22.6 120.3 all-gather.1
  152.4 18.6 reduce-scatter.1
where the time goes:
time: 193 us; the launch traced here: 192 us
  waiting for transfers between devices  134 us (69%)
  other arithmetic  16.1 us (8%)
  between operations  13.5 us (7%)
  local copies, waits for them, and re-layouts  13.1 us (7%)
  matrix products  9.22 us (5%)
  starting transfers between devices  6.42 us (3%)
    all_gather x1, waiting for transfers between devices, on_device(): gathered = lax.all_gather(folded, 'row', axis=1, tiled=True)  110 us
    reduce_scatter x1, waiting for transfers between devices, on_device(): piece = lax.psum_scatter(partial, 'col', scatter_dimension=2, tiled=True)  17.4 us
    dot_general x1, other arithmetic, on_device(): lax.dot_general(amp_kept, gathered, (((1, 3), (0, 1)), ((), ())), preferr...  10.7 us
    dot_general x1, matrix products, on_device(): lax.dot_general(amp_kept, gathered, (((1, 3), (0, 1)), ((), ())), preferr...  9.22 us
    ppermute x2, waiting for transfers between devices, on_device(): routes.append(lax.ppermute(piece, ('row', 'col'), pairs))  7.05 us
    ppermute x2, starting transfers between devices, on_device(): routes.append(lax.ppermute(piece, ('row', 'col'), pairs))  6.37 us
    unnamed x12, local copies, waits for them, and re-layouts  5.25 us
  transfers between devices with their start and end apart: 4, of which 4 were waited for; matrix products, arithmetic and copies ran while one was open for 6% of the time, Pallas kernels for 0%

commit v1 on v0

--- a/solution.py
+++ b/solution.py
@@ -2,6 +2,24 @@
 import jax.numpy as jnp
 from jax import lax
 from jax.sharding import PartitionSpec as P
+
+
+def ring_gather(array, axis, dim):
+    ways, here, step = (lax.axis_size(axis), lax.axis_index(axis), array.shape[dim])
+    lengths = [n * ways if d == dim else n for d, n in enumerate(array.shape)]
+    full = lax.dynamic_update_slice_in_dim(
+        jnp.zeros(lengths, array.dtype), array, here * step, axis=dim
+    )
+    going_up = going_down = array
+    for far in range(1, ways // 2 + 1):
+        going_up = lax.ppermute(going_up, axis, [(d, (d + 1) % ways) for d in range(ways)])
+        full = lax.dynamic_update_slice_in_dim(full, going_up, (here - far) % ways * step, axis=dim)
+        if 2 * far < ways:
+            going_down = lax.ppermute(going_down, axis, [(d, (d - 1) % ways) for d in range(ways)])
+            full = lax.dynamic_update_slice_in_dim(
+                full, going_down, (here + far) % ways * step, axis=dim
+            )
+    return full
 
 
 def folded_integrals(integrals, occ_local, vir_local, vir_irrep, screen_rows, pair_label):
@@ -31,7 +49,7 @@
     screen_rows = lax.dynamic_slice_in_dim(screen, occ_offset, occ_share, 0)
     pair_label = occ_irrep[batch_size]
     folded = folded_integrals(integrals, occ_local, vir_local, vir_irrep, screen_rows, pair_label)
-    gathered = lax.all_gather(folded, "row", axis=1, tiled=True)
+    gathered = ring_gather(folded, "row", 1)
     shift = jnp.bitwise_xor(occ_irrep[:batch_size, None], occ_local[None, :])
     keep_amp = (
         jnp.bitwise_xor(shift[:, :, None], vir_local[None, None, :])[:, :, :, None]

time: 193 us -> 180 us (0.933)
  waiting for transfers between devices: 134 us -> 105 us
  local copies, waits for them, and re-layouts: 13.1 us -> 24.8 us
  starting transfers between devices: 6.42 us -> 10.3 us
    all_gather x1 -> x0, waiting for transfers between devices: 110 us -> none  [on_device(): gathered = lax.all_gather(folded, 'row', axis=1, tiled=True)]
    ppermute x0 -> x3, waiting for transfers between devices: none -> 79.4 us  [the longest x2 59.1 us: ring_gather(): lax.ppermute(going_up, axis, [(d, (d + 1) % ways) for d in range(ways)])]
    ppermute x0 -> x3, local copies, waits for them, and re-layouts: none -> 9.35 us  [the longest x2 6.23 us: ring_gather(): lax.ppermute(going_up, axis, [(d, (d + 1) % ways) for d in range(ways)])]
    dynamic_update_slice x0 -> x4, local copies, waits for them, and re-layouts: none -> 5.42 us  [the longest x2 2.74 us: ring_gather(): lax.dynamic_update_slice_in_dim(full, going_up, (here - far) % ways * ste...]
    unnamed x12 -> x10, local copies, waits for them, and re-layouts: 5.25 us -> 0.02 us
    ppermute x0 -> x3, starting transfers between devices: none -> 3.88 us  [the longest x1 2.25 us: ring_gather(): lax.ppermute(going_down, axis, [(d, (d - 1) % ways) for d in range(ways)])]
    slice x1 -> x0, local copies, waits for them, and re-layouts: 3.42 us -> none  [folded_integrals(): integrals[:, :, :half]]
    broadcast_in_dim x0 -> x1, local copies, waits for them, and re-layouts: none -> 3.41 us  [ring_gather(): jnp.zeros(lengths, array.dtype)]
  transfers between devices with their start and end apart: 4 -> 6, of which waited for: 4 -> 6; matrix products, arithmetic and copies ran while one was open for 6% -> 16% of each run, Pallas kernels for 0% -> 0%
where the time goes in v1:
time: 180 us; the launch traced here: 179 us
  waiting for transfers between devices  105 us (58%)
  local copies, waits for them, and re-layouts  24.8 us (14%)
  other arithmetic  16.4 us (9%)
  between operations  13.5 us (8%)
  starting transfers between devices  10.3 us (6%)
  matrix products  9.24 us (5%)
    ppermute x2, waiting for transfers between devices, ring_gather(): lax.ppermute(going_up, axis, [(d, (d + 1) % ways) for d in range(ways)])  59.1 us
    ppermute x1, waiting for transfers between devices, ring_gather(): lax.ppermute(going_down, axis, [(d, (d - 1) % ways) for d in range(ways)])  20.2 us
    reduce_scatter x1, waiting for transfers between devices, on_device(): piece = lax.psum_scatter(partial, 'col', scatter_dimension=2, tiled=True)  18.6 us
    dot_general x1, other arithmetic, on_device(): lax.dot_general(amp_kept, gathered, (((1, 3), (0, 1)), ((), ())), preferr...  10.5 us
    dot_general x1, matrix products, on_device(): lax.dot_general(amp_kept, gathered, (((1, 3), (0, 1)), ((), ())), preferr...  9.24 us
    ppermute x2, waiting for transfers between devices, on_device(): routes.append(lax.ppermute(piece, ('row', 'col'), pairs))  7.03 us
    ppermute x2, starting transfers between devices, on_device(): routes.append(lax.ppermute(piece, ('row', 'col'), pairs))  6.39 us
    ppermute x2, local copies, waits for them, and re-layouts, ring_gather(): lax.ppermute(going_up, axis, [(d, (d + 1) % ways) for d in range(ways)])  6.23 us
  transfers between devices with their start and end apart: 6, of which 6 were waited for; matrix products, arithmetic and copies ran while one was open for 16% of the time, Pallas kernels for 0%

profile of v1, /device:TPU:2, one launch (start us, length us, event | category | flops | bytes accessed | tf_op | source)
XLA Modules:
  0.0 179.2 jit_solution(16281473984480083370)
XLA Ops:
  6.5 0.0 copy-start
  6.5 0.0 reduce-scatter.2.cloned.1.call-start
  6.5 1.3 slice.26
  7.8 0.8 fusion.13
  8.6 1.5 dynamic-slice_xor_fusion
  10.1 0.7 dynamic_slice.20
  10.8 0.0 copy-done
  10.8 0.1 constant_dynamic-slice_fusion
  10.9 0.1 copy.14
  11.0 0.1 multiply_reduce_fusion
  11.1 0.7 xor_select_fusion
  11.8 2.4 %compare_select_fusion.3 = bf16[25,128,256]{2,1,0:T(8,128)(2,1)S(1)} fusion(bf16[25,128,512]{2,1,0:T(8,128)(2,1)} %param.8, s32[256]{0:T(256)S(1)} %get-tuple-element.12, s32[256]{0:T(256)S(1)} %get-tuple-element.11, s32[25,128]{1,0:T(8,128)S(1)} %xor_select_fusion), kind=kLoop, calls=%fused_computation.7 | loop fusion | flops 3276800 | bytes 4930048 | tf_op jit(solution)/shard_map/jit(_where)/select_n | solution.py:36
  14.3 0.0 copy-start.1
  14.3 1.6 collective-permute-start
  15.9 2.2 %collective-permute-start.1 = (bf16[25,128,256]{2,1,0:T(8,128)(2,1)S(1)}, bf16[25,128,256]{2,1,0:T(8,128)(2,1)}, u32[]{:S(2)}, u32[]{:S(2)}) collective-permute-start(bf16[25,128,256]{2,1,0:T(8,128)(2,1)S(1)} %compare_select_fusion.3), channel_id=1, source_target_pairs={{0,12},{4,0},{8,4},{12,8},{1,13},{5,1},{9,5},{13,9},{2,14},{6,2},{... | collective-permute-start | bytes 4915208 | tf_op jit(solution)/shard_map/ppermute | solution.py:18
  18.1 2.1 %copy.15 = bf16[25,128,256]{1,2,0:T(8,128)(2,1)S(1)} copy(bf16[25,128,256]{2,1,0:T(8,128)(2,1)S(1)} %compare_select_fusion.3) | data formatting | bytes 3276800 | tf_op jit(solution)/shard_map/jit(_where)/select_n | solution.py:36
  20.3 0.0 copy-done.2
  20.3 0.1 broadcast_xor_fusion.1
  20.3 0.1 broadcast_xor_fusion
  20.4 3.4 %broadcast_in_dim.16 = bf16[25,512,256]{1,2,0:T(8,128)(2,1)} broadcast(bf16[]{:T(256)} %constant.57.clone.1), dimensions={} | broadcast | bytes 6553602 | tf_op jit(solution)/shard_map/broadcast_in_dim | solution.py:11
  23.8 1.4 constant_dynamic-update-slice_fusion.3
  25.2 29.7 %collective-permute-done = bf16[25,128,256]{2,1,0:T(8,128)(2,1)} collective-permute-done((bf16[25,128,256]{2,1,0:T(8,128)(2,1)S(1)}, bf16[25,128,256]{2,1,0:T(8,128)(2,1)}, u32[]{:S(2)}, u32[]{:S(2)}) %collective-permute-start) | collective-permute-done | bytes 1638432 | tf_op jit(solution)/shard_map/ppermute | solution.py:15
  55.0 0.0 collective-permute-start.2
  55.0 0.0 copy-done.1
  55.0 10.5 %compare_select_fusion.8 = bf16[4,25,128,512]{3,2,1,0:T(8,128)(2,1)} fusion(bf16[4,25,128,512]{3,2,1,0:T(8,128)(2,1)} %param.7, s32[512]{0:T(512)S(1)} %copy-done.1, s32[4,25,128]{2,1,0:T(8,128)S(1)} %broadcast_xor_fusion), kind=kLoop, calls=%fused_computation.clone.clone.clone.clone.1 | loop fusion | flops 13107200 | bytes 26267648 | tf_op jit(solution)/shard_map/dot_general | solution.py:59
  65.5 3.1 %copy.16 = bf16[25,128,256]{1,2,0:T(8,128)(2,1)S(1)} copy(bf16[25,128,256]{2,1,0:T(8,128)(2,1)} %collective-permute-done) | data formatting | bytes 3276800 | tf_op jit(solution)/shard_map/ppermute | solution.py:15
  68.6 20.2 %collective-permute-done.1 = bf16[25,128,256]{2,1,0:T(8,128)(2,1)} collective-permute-done((bf16[25,128,256]{2,1,0:T(8,128)(2,1)S(1)}, bf16[25,128,256]{2,1,0:T(8,128)(2,1)}, u32[]{:S(2)}, u32[]{:S(2)}) %collective-permute-start.1) | collective-permute-done | bytes 1638432 | tf_op jit(solution)/shard_map/ppermute | solution.py:18
  88.8 3.1 %copy.17 = bf16[25,128,256]{1,2,0:T(8,128)(2,1)S(1)} copy(bf16[25,128,256]{2,1,0:T(8,128)(2,1)} %collective-permute-done.1) | data formatting | bytes 3276800 | tf_op jit(solution)/shard_map/ppermute | solution.py:18
  92.0 1.4 constant_dynamic-update-slice_fusion.2
  93.4 1.3 constant_dynamic-update-slice_fusion.1
  94.7 29.4 %collective-permute-done.2 = bf16[25,128,256]{2,1,0:T(8,128)(2,1)} collective-permute-done((bf16[25,128,256]{2,1,0:T(8,128)(2,1)}, bf16[25,128,256]{2,1,0:T(8,128)(2,1)}, u32[]{:S(2)}, u32[]{:S(2)}) %collective-permute-start.2) | collective-permute-done | bytes 1638432 | tf_op jit(solution)/shard_map/ppermute | solution.py:15
  124.1 3.1 %copy.18 = bf16[25,128,256]{1,2,0:T(8,128)(2,1)S(1)} copy(bf16[25,128,256]{2,1,0:T(8,128)(2,1)} %collective-permute-done.2) | data formatting | bytes 3276800 | tf_op jit(solution)/shard_map/ppermute | solution.py:15
  127.2 1.3 constant_dynamic-update-slice_fusion
  128.6 9.2 %fusion.5 = f32[4,128,256]{1,2,0:T(8,128)} fusion(bf16[25,512,256]{1,2,0:T(8,128)(2,1)} %constant_dynamic-update-slice_fusion, bf16[4,25,128,512]{3,2,1,0:T(8,128)(2,1)} %compare_select_fusion.8), kind=kOutput, calls=%fused_computation.8 | convolution fusion | flops 3355443200 | bytes 20185088 | tf_op jit(solution)/shard_map/dot_general | solution.py:59
  137.8 0.0 reduce-scatter.2.cloned.1.call-update
  137.8 0.0 copy-done.4
  137.8 0.6 slice.32
  138.4 0.1 fusion.12
  138.5 0.6 slice_add_fusion
  139.2 0.1 broadcast_xor_fusion.2
  139.2 18.6 %reduce-scatter.2.cloned.1.call-done = f32[4,128,64]{1,2,0:T(8,128)} async-done(((f32[4,128,256]{1,2,0:T(8,128)}), f32[4,128,64]{1,2,0:T(8,128)}) %reduce-scatter.2.cloned.1.call-update) | async-done | bytes 131088 | tf_op jit(solution)/shard_map/reduce_scatter | solution.py:63
  157.8 4.5 %collective-permute-start.3 = (f32[4,128,64]{1,2,0:T(8,128)}, f32[4,128,64]{1,2,0:T(8,128)S(1)}, u32[]{:S(2)}, u32[]{:S(2)}) collective-permute-start(f32[4,128,64]{1,2,0:T(8,128)} %reduce-scatter.2.cloned.1.call-done), channel_id=1, source_target_pairs={{0,8},{1,0},{2,12},{3,4},{4,9},{5,1},{6,13},{7,5},{8,10},{9,2},{10... | collective-permute-start | bytes 393224 | tf_op jit(solution)/shard_map/ppermute | solution.py:71
  162.3 1.9 %collective-permute-start.4 = (f32[4,128,64]{1,2,0:T(8,128)}, f32[4,128,64]{1,2,0:T(8,128)S(1)}, u32[]{:S(2)}, u32[]{:S(2)}) collective-permute-start(f32[4,128,64]{1,2,0:T(8,128)} %reduce-scatter.2.cloned.1.call-done), channel_id=1, source_target_pairs={{0,0},{1,8},{2,4},{3,12},{4,1},{5,9},{6,5},{7,13},{8,2},{9,10},{10... | collective-permute-start | bytes 393224 | tf_op jit(solution)/shard_map/ppermute | solution.py:71
  164.2 0.1 broadcast_subtract_fusion
  164.3 1.4 collective-permute-done.3
  165.7 5.6 %collective-permute-done.4 = f32[4,128,64]{1,2,0:T(8,128)S(1)} collective-permute-done((f32[4,128,64]{1,2,0:T(8,128)}, f32[4,128,64]{1,2,0:T(8,128)S(1)}, u32[]{:S(2)}, u32[]{:S(2)}) %collective-permute-start.4) | collective-permute-done | bytes 131104 | tf_op jit(solution)/shard_map/ppermute | solution.py:71
  171.3 0.1 fusion.9
  171.5 0.9 copy.19
  (6 shorter events, 0.0 us)
Async XLA Ops:
  6.5 4.3 %copy-start = (s32[100,8]{0,1:T(8,128)S(1)}, s32[100,8]{0,1:T(8,128)}, u32[]{:S(2)}) copy-start(s32[100,8]{0,1:T(8,128)} %param.11) | copy-start | bytes 9604
  6.5 13.7 %copy-start.2 = (s32[100]{0:T(128)S(1)}, s32[100]{0:T(128)}, u32[]{:S(2)}) copy-start(s32[100]{0:T(128)} %param.9) | copy-start | bytes 1204
  6.5 151.3 %reduce-scatter.2.cloned.1.call-start = ((), (), s32[]{:S(2)}) async-start(), calls=%async_computation.1 | async-start | bytes 655360 | tf_op jit(solution)/shard_map/reduce_scatter | solution.py:63
  14.3 40.7 %copy-start.1 = (s32[512]{0:T(512)S(1)}, s32[512]{0:T(512)}, u32[]{:S(2)}) copy-start(s32[512]{0:T(512)} %param.10) | copy-start | bytes 6148
  14.3 40.7 %collective-permute-start = (bf16[25,128,256]{2,1,0:T(8,128)(2,1)S(1)}, bf16[25,128,256]{2,1,0:T(8,128)(2,1)}, u32[]{:S(2)}, u32[]{:S(2)}) collective-permute-start(bf16[25,128,256]{2,1,0:T(8,128)(2,1)S(1)} %compare_select_fusion.3), channel_id=1, source_target_pairs={{0,4},{4,8},{8,12},{12,0},{1,5},{5,9},{9,13},{13,1},{2,6},{6,10},{... | collective-permute-start | bytes 4915208 | tf_op jit(solution)/shard_map/ppermute | solution.py:15
  15.9 72.9 %collective-permute-start.1 = (bf16[25,128,256]{2,1,0:T(8,128)(2,1)S(1)}, bf16[25,128,256]{2,1,0:T(8,128)(2,1)}, u32[]{:S(2)}, u32[]{:S(2)}) collective-permute-start(bf16[25,128,256]{2,1,0:T(8,128)(2,1)S(1)} %compare_select_fusion.3), channel_id=1, source_target_pairs={{0,12},{4,0},{8,4},{12,8},{1,13},{5,1},{9,5},{13,9},{2,14},{6,2},{... | collective-permute-start | bytes 4915208 | tf_op jit(solution)/shard_map/ppermute | solution.py:18
  55.0 69.1 %collective-permute-start.2 = (bf16[25,128,256]{2,1,0:T(8,128)(2,1)}, bf16[25,128,256]{2,1,0:T(8,128)(2,1)}, u32[]{:S(2)}, u32[]{:S(2)}) collective-permute-start(bf16[25,128,256]{2,1,0:T(8,128)(2,1)} %collective-permute-done), channel_id=1, source_target_pairs={{0,4},{4,8},{8,12},{12,0},{1,5},{5,9},{9,13},{13,1},{2,6},{6,10},{... | collective-permute-start | bytes 4915208 | tf_op jit(solution)/shard_map/ppermute | solution.py:15
  128.6 9.3 %copy-start.4 = (f32[100]{0:T(128)S(1)}, f32[100]{0:T(128)}, u32[]{:S(2)}) copy-start(f32[100]{0:T(128)} %param.12) | copy-start | bytes 1204
  128.6 9.9 %copy-start.3 = (f32[512]{0:T(512)S(1)}, f32[512]{0:T(512)}, u32[]{:S(2)}) copy-start(f32[512]{0:T(512)} %param.13) | copy-start | bytes 6148
  157.8 7.9 %collective-permute-start.3 = (f32[4,128,64]{1,2,0:T(8,128)}, f32[4,128,64]{1,2,0:T(8,128)S(1)}, u32[]{:S(2)}, u32[]{:S(2)}) collective-permute-start(f32[4,128,64]{1,2,0:T(8,128)} %reduce-scatter.2.cloned.1.call-done), channel_id=1, source_target_pairs={{0,8},{1,0},{2,12},{3,4},{4,9},{5,1},{6,13},{7,5},{8,10},{9,2},{10... | collective-permute-start | bytes 393224 | tf_op jit(solution)/shard_map/ppermute | solution.py:71
  162.3 9.0 %collective-permute-start.4 = (f32[4,128,64]{1,2,0:T(8,128)}, f32[4,128,64]{1,2,0:T(8,128)S(1)}, u32[]{:S(2)}, u32[]{:S(2)}) collective-permute-start(f32[4,128,64]{1,2,0:T(8,128)} %reduce-scatter.2.cloned.1.call-done), channel_id=1, source_target_pairs={{0,0},{1,8},{2,4},{3,12},{4,1},{5,9},{6,5},{7,13},{8,2},{9,10},{10... | collective-permute-start | bytes 393224 | tf_op jit(solution)/shard_map/ppermute | solution.py:71
Sparse Core Ops, SparseCore 0:
  137.9 19.8 reduce-scatter.1
